TPU v7x, 32 devices: a whole 2x2x4 slice. The times are simulated.
32 devices in a mesh: cons: 4 (over y, core), prod: 8 (over z, x).
Axes of the slice: x: 2, y: 2, z: 4, core: 2. Of those that a mesh axis runs over, the one named last changes fastest.
Arguments:
- tastes: bfloat16 [16384, 128], P('cons'), may hold values from -128 to 128
- price_coef: float32 [16384], P('cons'), may hold values from 0.5 to 5
- characteristics: bfloat16 [16384, 128], P('prod'), may hold values from -6 to 6
- mean_utility: float32 [16384], P('prod'), may hold values from -4 to 4
- panel_cols: int32 [256], replicated, may hold values from 0 to 16383
- firm_map: int32 [16384], P('prod'), may hold values from 0 to 16383, as said below
- inverses: float32 [128, 128, 128], P('prod'), may hold values from -0.5 to 0.5
Outputs:
- shares: float32 [16384], P('prod')
- markup: float32 [16384], P('prod')
- response: float32 [16384, 256], P('prod')
Inputs may be any that keep to these rules, and one draw needn't show every extreme that they name: `firm_map`: a permutation of the products; the rows of firm order held by each index of prod name exactly 256 products held by each index of prod.
All inputs are finite; a program needn't handle non-finite values.
Results may differ from a plain program's by a relative error of at most 0.002.
The roundings to bfloat16 on the way count: a program that leaves them out, or rounds other values in their place, can miss the bound.
Values may be sent and summed in bfloat16 or wider, within the bound.
A program may use at most 64 MiB of HBM per device.

v0:
```python
import jax
import jax.numpy as jnp
from jax import lax
from jax.sharding import PartitionSpec as P


def utilities(taste_block, characteristics, mean_utility):
    return (
        jnp.einsum("ik,jk->ij", taste_block, characteristics, preferred_element_type=jnp.float32)
        + mean_utility[None, :]
    )


def request_order(firm_map):
    local_count = firm_map.shape[0]
    holders = lax.axis_size("prod")
    per_pair = local_count // holders
    source = firm_map // local_count
    order = jnp.argsort(source, stable=True)
    wanted = firm_map[order].reshape(holders, per_pair)
    return (order, wanted)


def regroup(jacobian, shares, firm_map):
    local_count = jacobian.shape[0]
    order, wanted = request_order(firm_map)
    base = lax.axis_index("prod") * local_count
    local_ids = lax.all_to_all(wanted, "prod", split_axis=0, concat_axis=0, tiled=True) - base
    rows_out = jnp.take(jacobian, local_ids, axis=0)
    values_out = jnp.take(shares, local_ids, axis=0)
    rows_back = lax.all_to_all(rows_out, "prod", split_axis=0, concat_axis=0, tiled=True)
    values_back = lax.all_to_all(values_out, "prod", split_axis=0, concat_axis=0, tiled=True)
    flat_rows = rows_back.reshape(local_count, jacobian.shape[1])
    flat_values = values_back.reshape(local_count)
    placed_rows = jnp.zeros_like(flat_rows).at[order].set(flat_rows)
    placed_values = jnp.zeros_like(flat_values).at[order].set(flat_values)
    return (placed_rows, placed_values)


def apply_blocks(inverses, placed_rows, placed_values):
    firm_count, block_size = (inverses.shape[0], inverses.shape[1])
    ordered = placed_rows.reshape(firm_count, block_size, placed_rows.shape[1])
    response = jnp.einsum(
        "fab,fbc->fac", inverses, ordered, precision=lax.Precision.HIGHEST
    ).reshape(placed_rows.shape)
    markup = jnp.einsum(
        "fab,fb->fa",
        inverses,
        placed_values.reshape(firm_count, block_size),
        precision=lax.Precision.HIGHEST,
    ).reshape(placed_values.shape)
    return (response, markup)


def body(tastes, price_coef, characteristics, mean_utility, panel_cols, firm_map, inverses):
    local_products = characteristics.shape[0]
    local_consumers = tastes.shape[0]
    col_count = panel_cols.shape[0]
    count_products = local_products * lax.axis_size("prod")
    count_consumers = local_consumers * lax.axis_size("cons")
    product_ids = lax.axis_index("prod") * local_products + lax.iota(jnp.int32, local_products)
    hits = product_ids[None, :] == panel_cols[:, None]
    part_chars = jnp.dot(
        hits.astype(jnp.bfloat16), characteristics, preferred_element_type=jnp.float32
    )
    part_means = jnp.dot(hits.astype(jnp.float32), mean_utility, precision=lax.Precision.HIGHEST)
    col_chars, col_means = lax.psum((part_chars, part_means), "prod")
    used_chars, used_means, used_ids = (characteristics, mean_utility, product_ids)
    block_rows = min(512, local_consumers)
    block_count = local_consumers // block_rows
    taste_blocks = tastes.reshape(block_count, block_rows, tastes.shape[1])
    coef_blocks = price_coef.reshape(block_count, block_rows)

    def local_peak(taste_block):
        utility = utilities(taste_block, used_chars, used_means)
        return jnp.maximum(jnp.max(utility, axis=1), 0.0)

    highest = lax.pmax(lax.map(local_peak, taste_blocks).reshape(local_consumers), "prod")

    def local_sum(inputs):
        taste_block, peak_block = inputs
        utility = utilities(taste_block, used_chars, used_means)
        return jnp.sum(jnp.exp(utility - peak_block[:, None]), axis=1)

    partial_total = lax.map(local_sum, (taste_blocks, highest.reshape(block_count, block_rows)))
    total = lax.psum(partial_total.reshape(local_consumers), "prod")
    denominator = jnp.exp(-highest) + total

    def consume(state_now, inputs):
        panel_sum, share_sum, diag_sum = state_now
        taste_block, coef_block, peak_block, denom_block = inputs
        utility = utilities(taste_block, used_chars, used_means)
        scaled = count_products * jnp.exp(utility - peak_block[:, None]) / denom_block[:, None]
        share_sum = share_sum + jnp.sum(scaled, axis=0)
        diag_sum = diag_sum + jnp.dot(coef_block, scaled, precision=lax.Precision.HIGHEST)
        col_util = (
            jnp.dot(taste_block.astype(jnp.float32), col_chars.T, precision=lax.Precision.HIGHEST)
            + col_means[None, :]
        )
        col_scaled = count_products * jnp.exp(col_util - peak_block[:, None]) / denom_block[:, None]
        weighted = (coef_block[:, None] * col_scaled).astype(jnp.bfloat16)
        panel_sum = panel_sum + lax.dot_general(
            scaled.astype(jnp.bfloat16),
            weighted,
            (((0,), (0,)), ((), ())),
            preferred_element_type=jnp.float32,
        )
        return ((panel_sum, share_sum, diag_sum), None)

    start_state = (
        jnp.zeros((local_products, col_count), jnp.float32),
        jnp.zeros((local_products,), jnp.float32),
        jnp.zeros((local_products,), jnp.float32),
    )
    scan_inputs = (
        taste_blocks,
        coef_blocks,
        highest.reshape(block_count, block_rows),
        denominator.reshape(block_count, block_rows),
    )
    (panel_sum, share_sum, diag_sum), _ = lax.scan(consume, start_state, scan_inputs)
    marks = (used_ids[:, None] == panel_cols[None, :]).astype(jnp.float32)
    part_cols = col_count // lax.axis_size("cons")
    panel_part = lax.psum_scatter(panel_sum, "cons", scatter_dimension=1, tiled=True)
    share_all, diag_all = lax.psum((share_sum, diag_sum), "cons")
    mark_part = lax.dynamic_slice_in_dim(marks, lax.axis_index("cons") * part_cols, part_cols, 1)
    local_shares = share_all / count_consumers
    diagonal = diag_all / count_consumers
    jacobian = panel_part / count_consumers - diagonal[:, None] * mark_part
    placed_rows, placed_values = regroup(jacobian, local_shares, firm_map)
    response, markup = apply_blocks(inverses, placed_rows, placed_values)
    response = lax.all_gather(response, "cons", axis=1, tiled=True)
    return (local_shares, markup, response)


def solution(mesh):
    return jax.shard_map(
        body,
        mesh=mesh,
        in_specs=(
            P("cons", None),
            P("cons"),
            P("prod", None),
            P("prod"),
            P(),
            P("prod"),
            P("prod", None, None),
        ),
        out_specs=(P("prod"), P("prod"), P("prod", None)),
        check_vma=False,
    )
```

profile of v0, /device:TPU:0, one launch (start us, length us, event | category | flops | bytes accessed | tf_op | source)
XLA Modules:
  0.0 332.7 jit_solution(9404396025365228283)
XLA Ops:
  9.6 15.6 %while.35 = (s32[]{:T(128)}, f32[8,512]{1,0:T(8,128)S(1)}, bf16[8,512,128]{2,1,0:T(8,128)(2,1)}, bf16[2048,128]{1,0:T(8,128)(2,1)}, f32[2048]{0:T(1024)}, /*index=5*/s32[]{:T(128)}, s32[]{:T(128)}) while((s32[]{:T(128)}, f32[8,512]{1,0:T(8,128)S(1)}, bf16[8,512,128]{2,1,0:T(8,128)(2,1)}, bf16[2048,128]{1,0:T(8,128)(2,1)}, f32[2048]{0:T(1024)}, ...), condition=%wide.region_2.3_spmd, body=%wide.region_0.2_spmd.sunk | while | flops 270532608 | bytes 674385 | solution.py:78
  25.3 38.9 %pmax.7 = f32[4096]{0:T(1024)S(1)} all-reduce(f32[4096]{0:T(1024)S(1)} %bitcast.120), channel_id=1, replica_groups=mesh['cons'=4,'prod'=8] {'prod'}, use_global_device_ids=true, to_apply=%region_3.0 | all-reduce | flops 4096 | bytes 32768 | tf_op jit(solution)/shard_map/pmax | solution.py:78
  64.1 16.9 %while.36 = (s32[]{:T(128)}, f32[8,512]{1,0:T(8,128)S(1)}, bf16[8,512,128]{2,1,0:T(8,128)(2,1)}, bf16[2048,128]{1,0:T(8,128)(2,1)}, f32[2048]{0:T(1024)}, /*index=5*/f32[8,512]{1,0:T(8,128)S(1)}, s32[]{:T(128)}, s32[]{:T(128)}) while((s32[]{:T(128)}, f32[8,512]{1,0:T(8,128)S(1)}, bf16[8,512,128]{2,1,0:T(8,128)(2,1)}, ...), condition=%wide.region_6.7_spmd, body=%wide.region_4.6_spmd.sunk | while | flops 271580672 | bytes 676445 | solution.py:85
  82.8 33.0 %all-reduce = (f32[4096]{0:T(1024)S(1)}, f32[256]{0:T(256)S(1)}) all-reduce(f32[4096]{0:T(1024)S(1)} %bitcast.119, f32[256]{0:T(256)S(1)} %bitcast.132), channel_id=1, replica_groups=mesh['cons'=4,'prod'=8] {'prod'}, use_global_device_ids=true, to_apply=%region_7.8 | all-reduce | flops 4352 | bytes 34816 | tf_op jit(solution)/shard_map/psum | solution.py:86
  115.9 93.8 %while.37 = (s32[]{:T(128)}, f32[2048,256]{1,0:T(8,128)S(1)}, f32[2048]{0:T(1024)S(1)}, f32[2048]{0:T(1024)S(1)}, bf16[8,512,128]{2,1,0:T(8,128)(2,1)}, /*index=...) while((s32[]{:T(128)}, f32[2048,256]{1,0:T(8,128)S(1)}, ...), condition=%wide.region_12.13_spmd.clone, body=%wide.region_10.12_spmd.clone.sunk | while | flops 1027348480 | bytes 35621072 | solution.py:121
  123.6 4.0 %convolution_add_fusion.3 = f32[2048,256]{1,0:T(8,128)S(1)} fusion(bf16[512,256]{1,0:T(8,128)(2,1)S(1)} %fusion.74, f32[2048,256]{1,0:T(8,128)S(1)} %get-tuple-element.451, f32[512,2048]{1,0:T(8,128)} %copy-done.3, pred[]{:T(512)S(6)} %compare.9), kind=kOutput, calls=%fused_computation.16.clone.1 | convolution fusion | flops 538968064 | bytes 8650753 | tf_op jit(solution)/shard_map/while/body/eval_jaxpr/dot_general | solution.py:102
  135.3 4.0 %convolution_add_fusion.3 = f32[2048,256]{1,0:T(8,128)S(1)} fusion(bf16[512,256]{1,0:T(8,128)(2,1)S(1)} %fusion.74, f32[2048,256]{1,0:T(8,128)S(1)} %get-tuple-element.451, f32[512,2048]{1,0:T(8,128)} %copy-done.3, pred[]{:T(512)S(6)} %compare.9), kind=kOutput, calls=%fused_computation.16.clone.1 | convolution fusion | flops 538968064 | bytes 8650753 | tf_op jit(solution)/shard_map/while/body/eval_jaxpr/dot_general | solution.py:102
  147.0 4.0 %convolution_add_fusion.3 = f32[2048,256]{1,0:T(8,128)S(1)} fusion(bf16[512,256]{1,0:T(8,128)(2,1)S(1)} %fusion.74, f32[2048,256]{1,0:T(8,128)S(1)} %get-tuple-element.451, f32[512,2048]{1,0:T(8,128)} %copy-done.3, pred[]{:T(512)S(6)} %compare.9), kind=kOutput, calls=%fused_computation.16.clone.1 | convolution fusion | flops 538968064 | bytes 8650753 | tf_op jit(solution)/shard_map/while/body/eval_jaxpr/dot_general | solution.py:102
  158.8 4.0 %convolution_add_fusion.3 = f32[2048,256]{1,0:T(8,128)S(1)} fusion(bf16[512,256]{1,0:T(8,128)(2,1)S(1)} %fusion.74, f32[2048,256]{1,0:T(8,128)S(1)} %get-tuple-element.451, f32[512,2048]{1,0:T(8,128)} %copy-done.3, pred[]{:T(512)S(6)} %compare.9), kind=kOutput, calls=%fused_computation.16.clone.1 | convolution fusion | flops 538968064 | bytes 8650753 | tf_op jit(solution)/shard_map/while/body/eval_jaxpr/dot_general | solution.py:102
  170.5 4.0 %convolution_add_fusion.3 = f32[2048,256]{1,0:T(8,128)S(1)} fusion(bf16[512,256]{1,0:T(8,128)(2,1)S(1)} %fusion.74, f32[2048,256]{1,0:T(8,128)S(1)} %get-tuple-element.451, f32[512,2048]{1,0:T(8,128)} %copy-done.3, pred[]{:T(512)S(6)} %compare.9), kind=kOutput, calls=%fused_computation.16.clone.1 | convolution fusion | flops 538968064 | bytes 8650753 | tf_op jit(solution)/shard_map/while/body/eval_jaxpr/dot_general | solution.py:102
  182.2 4.0 %convolution_add_fusion.3 = f32[2048,256]{1,0:T(8,128)S(1)} fusion(bf16[512,256]{1,0:T(8,128)(2,1)S(1)} %fusion.74, f32[2048,256]{1,0:T(8,128)S(1)} %get-tuple-element.451, f32[512,2048]{1,0:T(8,128)} %copy-done.3, pred[]{:T(512)S(6)} %compare.9), kind=kOutput, calls=%fused_computation.16.clone.1 | convolution fusion | flops 538968064 | bytes 8650753 | tf_op jit(solution)/shard_map/while/body/eval_jaxpr/dot_general | solution.py:102
  193.9 4.0 %convolution_add_fusion.3 = f32[2048,256]{1,0:T(8,128)S(1)} fusion(bf16[512,256]{1,0:T(8,128)(2,1)S(1)} %fusion.74, f32[2048,256]{1,0:T(8,128)S(1)} %get-tuple-element.451, f32[512,2048]{1,0:T(8,128)} %copy-done.3, pred[]{:T(512)S(6)} %compare.9), kind=kOutput, calls=%fused_computation.16.clone.1 | convolution fusion | flops 538968064 | bytes 8650753 | tf_op jit(solution)/shard_map/while/body/eval_jaxpr/dot_general | solution.py:102
  205.6 4.0 %convolution_add_fusion.3 = f32[2048,256]{1,0:T(8,128)S(1)} fusion(bf16[512,256]{1,0:T(8,128)(2,1)S(1)} %fusion.74, f32[2048,256]{1,0:T(8,128)S(1)} %get-tuple-element.451, f32[512,2048]{1,0:T(8,128)} %copy-done.3, pred[]{:T(512)S(6)} %compare.9), kind=kOutput, calls=%fused_computation.16.clone.1 | convolution fusion | flops 538968064 | bytes 8650753 | tf_op jit(solution)/shard_map/while/body/eval_jaxpr/dot_general | solution.py:102
  211.5 5.0 %sort.17 = (s32[2048]{0:T(1024)}, s32[2048]{0:T(1024)S(1)}) sort(s32[2048]{0:T(1024)S(1)} %add_select_fusion, s32[2048]{0:T(1024)S(1)} %iota.12), dimensions={0}, to_apply=%region_14.15 | sort | flops 22528 | bytes 32768 | tf_op jit(solution)/shard_map/jit(argsort)/sort | solution.py:19
  216.6 20.5 %gather_fusion = s32[2048]{0:T(1024)} fusion(s32[2048]{0:T(1024)S(1)} %copy-done.1, s32[2048]{0:T(1024)S(1)} %get-tuple-element.240), kind=kCustom, calls=%fused_computation | custom fusion | bytes 24576 | tf_op jit(solution)/shard_map/gather | solution.py:20
  237.1 3.3 %all-to-all-start = ((s32[8,1,256]{2,1,0:T(1,128)}), s32[8,1,256]{2,1,0:T(1,128)S(1)}, u32[]{:S(2)}, u32[]{:S(2)}) async-start(s32[8,1,256]{2,1,0:T(1,128)} %bitcast.8), calls=%async_computation | async-start | bytes 16384 | tf_op jit(solution)/shard_map/all_to_all | solution.py:28
  240.6 6.3 %all-to-all-done = s32[8,1,256]{2,1,0:T(1,128)S(1)} async-done(((s32[8,1,256]{2,1,0:T(1,128)}), s32[8,1,256]{2,1,0:T(1,128)S(1)}, u32[]{:S(2)}, u32[]{:S(2)}) %all-to-all-start) | async-done | bytes 8224 | tf_op jit(solution)/shard_map/all_to_all | solution.py:28
  247.0 10.3 %all-reduce.1 = (f32[2048]{0:T(1024)S(1)}, f32[2048]{0:T(1024)S(1)}) all-reduce(f32[2048]{0:T(1024)S(1)} %get-tuple-element.129, f32[2048]{0:T(1024)S(1)} %get-tuple-element.132), channel_id=1, replica_groups=mesh['cons'=4,'prod'=8] {'cons'}, use_global_device_ids=true, to_apply=%region_13.14 | all-reduce | flops 4096 | bytes 32768 | tf_op jit(solution)/shard_map/psum | solution.py:125
  259.4 5.5 %gather_fusion.2 = f32[2048,64]{1,0:T(8,128)S(1)} fusion(f32[2048,64]{1,0:T(8,128)S(1)} %multiply_subtract_fusion, s32[2048]{0:T(1024)S(1)} %broadcast_clamp_fusion), kind=kCustom, calls=%fused_computation.2 | custom fusion | bytes 1056768 | tf_op jit(solution)/shard_map/jit(_take)/gather | solution.py:29
  265.3 16.7 %all_to_all.20 = f32[8,256,64]{1,2,0:T(8,128)S(1)} all-to-all(f32[8,256,64]{1,2,0:T(8,128)S(1)} %broadcast_select_fusion), channel_id=1, replica_groups=mesh['cons'=4,'prod'=8] {'prod'}, dimensions={0} | all-to-all | bytes 1048576 | tf_op jit(solution)/shard_map/all_to_all | solution.py:31
  282.3 5.8 %scatter_custom_fusion.1 = f32[2048,64]{1,0:T(8,128)S(1)} fusion(s32[2048]{0:T(1024)S(1)} %get-tuple-element.241, f32[2048,64]{1,0:T(8,128)S(1)} %bitcast.112, f32[]{:T(128)} %constant.94.clone.1), kind=kCustom, calls=%fused_computation.49 | custom fusion | bytes 524292 | tf_op jit(solution)/shard_map/scatter | solution.py:35
  291.1 11.8 %gather_fusion.1 = f32[2048]{0:T(1024)S(1)} fusion(f32[2048]{0:T(1024)S(1)} %broadcast_multiply_fusion.1, s32[2048]{0:T(1024)S(1)} %broadcast_clamp_fusion), kind=kCustom, calls=%fused_computation.1 | custom fusion | bytes 24576 | tf_op jit(solution)/shard_map/jit(_take)/gather | solution.py:30
  302.9 9.9 %all_to_all.21 = f32[8,1,256]{2,1,0:T(1,128)S(1)} all-to-all(f32[8,1,256]{2,1,0:T(1,128)S(1)} %and_select_fusion), channel_id=1, replica_groups=mesh['cons'=4,'prod'=8] {'prod'}, dimensions={0} | all-to-all | bytes 16384 | tf_op jit(solution)/shard_map/all_to_all | solution.py:32
  312.8 8.0 %scatter_custom_fusion = f32[2048]{0:T(1024)S(1)} fusion(s32[2048]{0:T(1024)S(1)} %get-tuple-element.241, f32[2048]{0:T(1024)S(1)} %bitcast.131, f32[]{:T(128)} %constant.94.clone.1), kind=kCustom, calls=%fused_computation.72 | custom fusion | bytes 8196 | tf_op jit(solution)/shard_map/scatter | solution.py:36
  (189 shorter events, 110.3 us)
Async XLA Ops:
  7.2 281.0 %copy-start = (f32[16,128,128]{2,1,0:T(8,128)S(1)}, f32[16,128,128]{2,1,0:T(8,128)}, u32[]{:S(2)}) copy-start(f32[16,128,128]{2,1,0:T(8,128)} %param.19) | copy-start | bytes 3145732
  7.2 108.7 %all-reduce.4.cloned.1.call-start = ((), (), s32[]{:S(2)}) async-start(), calls=%async_computation.4 | async-start | bytes 262144 | tf_op jit(solution)/shard_map/psum | solution.py:67
  9.5 247.8 %reduce-scatter.4.cloned.1.call-start = ((), (), s32[]{:S(2)}) async-start(), calls=%async_computation.6 | async-start | bytes 2621440
  64.1 16.9 %copy-start.6 = (s32[256]{0:T(256)S(1)}, s32[256]{0:T(256)}, u32[]{:S(2)}) copy-start(s32[256]{0:T(256)} %param.17) | copy-start | bytes 3076
  64.1 51.7 %copy-start.4 = (f32[4096]{0:T(1024)S(1)}, f32[4096]{0:T(1024)}, u32[]{:S(2)}) copy-start(f32[4096]{0:T(1024)} %param.14) | copy-start | bytes 49156
  118.2 1.9 copy-start.3
  118.2 4.0 %copy-start.5 = (f32[256,128]{1,0:T(8,128)S(1)}, f32[256,128]{1,0:T(8,128)}, u32[]{:S(2)}) copy-start(f32[256,128]{1,0:T(8,128)} %get-tuple-element.474) | copy-start | bytes 393220 | tf_op jit(solution)/shard_map/while
  129.9 1.9 copy-start.3
  129.9 4.0 %copy-start.5 = (f32[256,128]{1,0:T(8,128)S(1)}, f32[256,128]{1,0:T(8,128)}, u32[]{:S(2)}) copy-start(f32[256,128]{1,0:T(8,128)} %get-tuple-element.474) | copy-start | bytes 393220 | tf_op jit(solution)/shard_map/while
  141.7 1.9 copy-start.3
  141.7 4.0 %copy-start.5 = (f32[256,128]{1,0:T(8,128)S(1)}, f32[256,128]{1,0:T(8,128)}, u32[]{:S(2)}) copy-start(f32[256,128]{1,0:T(8,128)} %get-tuple-element.474) | copy-start | bytes 393220 | tf_op jit(solution)/shard_map/while
  153.4 1.9 copy-start.3
  153.4 4.0 %copy-start.5 = (f32[256,128]{1,0:T(8,128)S(1)}, f32[256,128]{1,0:T(8,128)}, u32[]{:S(2)}) copy-start(f32[256,128]{1,0:T(8,128)} %get-tuple-element.474) | copy-start | bytes 393220 | tf_op jit(solution)/shard_map/while
  165.1 1.9 copy-start.3
  165.1 4.0 %copy-start.5 = (f32[256,128]{1,0:T(8,128)S(1)}, f32[256,128]{1,0:T(8,128)}, u32[]{:S(2)}) copy-start(f32[256,128]{1,0:T(8,128)} %get-tuple-element.474) | copy-start | bytes 393220 | tf_op jit(solution)/shard_map/while
  176.8 1.9 copy-start.3
  176.8 4.0 %copy-start.5 = (f32[256,128]{1,0:T(8,128)S(1)}, f32[256,128]{1,0:T(8,128)}, u32[]{:S(2)}) copy-start(f32[256,128]{1,0:T(8,128)} %get-tuple-element.474) | copy-start | bytes 393220 | tf_op jit(solution)/shard_map/while
  188.5 1.9 copy-start.3
  188.6 4.0 %copy-start.5 = (f32[256,128]{1,0:T(8,128)S(1)}, f32[256,128]{1,0:T(8,128)}, u32[]{:S(2)}) copy-start(f32[256,128]{1,0:T(8,128)} %get-tuple-element.474) | copy-start | bytes 393220 | tf_op jit(solution)/shard_map/while
  200.3 1.9 copy-start.3
  200.3 4.0 %copy-start.5 = (f32[256,128]{1,0:T(8,128)S(1)}, f32[256,128]{1,0:T(8,128)}, u32[]{:S(2)}) copy-start(f32[256,128]{1,0:T(8,128)} %get-tuple-element.474) | copy-start | bytes 393220 | tf_op jit(solution)/shard_map/while
  237.1 9.8 %all-to-all-start = ((s32[8,1,256]{2,1,0:T(1,128)}), s32[8,1,256]{2,1,0:T(1,128)S(1)}, u32[]{:S(2)}, u32[]{:S(2)}) async-start(s32[8,1,256]{2,1,0:T(1,128)} %bitcast.8), calls=%async_computation | async-start | bytes 16384 | tf_op jit(solution)/shard_map/all_to_all | solution.py:28
  240.5 82.8 %all-gather.2.cloned.1.call-start = ((), (), s32[]{:S(2)}) async-start(), calls=%async_computation.5 | async-start | bytes 2621440 | tf_op jit(solution)/shard_map/all_gather | solution.py:132
  291.1 11.8 %copy-start.2 = (f32[2048]{0:T(1024)}, f32[2048]{0:T(1024)S(1)}, u32[]{:S(2)}) copy-start(f32[2048]{0:T(1024)S(1)} %broadcast_multiply_fusion.1) | copy-start | bytes 24580
  (1 other events, 1.9 us)
Sparse Core Ops, SparseCore 0:
  11.9 73.2 all-reduce.3
  211.6 28.5 reduce-scatter.3
  291.2 20.6 all-gather.1
where the time goes:
time: 334 us; the launch traced here: 333 us
  matrix products  117 us (35%)
  blocking collectives  109 us (33%)
  local copies, waits for them, and re-layouts  75.8 us (23%)
  between operations  14.1 us (4%)
  waiting for transfers between devices  6.41 us (2%)
  other arithmetic  6 us (2%)
  starting transfers between devices  3.46 us (1%)
    dot_general x24, matrix products, utilities(): jnp.einsum('ik,jk->ij', taste_block, characteristics, preferred_element_t...  49.2 us
    pmax x1, blocking collectives, body(): lax.pmax(lax.map(local_peak, taste_blocks).reshape(local_consumers), 'prod')  38.9 us
    psum x1, blocking collectives, body(): total = lax.psum(partial_total.reshape(local_consumers), 'prod')  33 us
    dot_general x8, matrix products, consume(): lax.dot_general(scaled.astype(jnp.bfloat16), weighted, (((0,), (0,)), (()...  32 us
    gather x1, local copies, waits for them, and re-layouts, request_order(): wanted = firm_map[order].reshape(holders, per_pair)  20.5 us
    all_to_all x1, blocking collectives, regroup(): lax.all_to_all(rows_out, 'prod', split_axis=0, concat_axis=0, tiled=True)  16.7 us
    dot_general x8, matrix products, consume(): jnp.dot(coef_block, scaled, precision=lax.Precision.HIGHEST)  16.6 us
    while x32, local copies, waits for them, and re-layouts  15.2 us
  transfers between devices with their start and end apart: 4, of which 1 were waited for; matrix products, arithmetic and copies ran while one was open for 25% of the time, Pallas kernels for 0%

commit v1 on v0

--- a/solution.py
+++ b/solution.py
@@ -83,7 +83,9 @@
         return jnp.sum(jnp.exp(utility - peak_block[:, None]), axis=1)
 
     partial_total = lax.map(local_sum, (taste_blocks, highest.reshape(block_count, block_rows)))
-    total = lax.psum(partial_total.reshape(local_consumers), "prod")
+    x = partial_total.reshape(local_consumers)
+    terms = lax.all_gather(x, "prod", axis=0, tiled=False)
+    total = terms.sum(axis=0)
     denominator = jnp.exp(-highest) + total
 
     def consume(state_now, inputs):

time: 334 us -> 349 us (1.045)
  blocking collectives: 109 us -> 123 us
    all_gather x0 -> x1, blocking collectives: none -> 30.5 us  [body(): terms = lax.all_gather(x, 'prod', axis=0, tiled=False)]
    psum x1, blocking collectives: 33 us -> 17.2 us  [body(): col_chars, col_means = lax.psum((part_chars, part_means), 'prod')]
  transfers between devices with their start and end apart: 4 -> 4, of which waited for: 1 -> 1; matrix products, arithmetic and copies ran while one was open for 25% -> 24% of each run, Pallas kernels for 0% -> 0%
where the time goes in v1:
time: 349 us; the launch traced here: 347 us
  blocking collectives  123 us (35%)
  matrix products  117 us (34%)
  local copies, waits for them, and re-layouts  75.8 us (22%)
  between operations  14.1 us (4%)
  waiting for transfers between devices  6.39 us (2%)
  other arithmetic  6.1 us (2%)
    dot_general x24, matrix products, utilities(): jnp.einsum('ik,jk->ij', taste_block, characteristics, preferred_element_t...  49.3 us
    pmax x1, blocking collectives, body(): lax.pmax(lax.map(local_peak, taste_blocks).reshape(local_consumers), 'prod')  38.9 us
    dot_general x8, matrix products, consume(): lax.dot_general(scaled.astype(jnp.bfloat16), weighted, (((0,), (0,)), (()...  32 us
    all_gather x1, blocking collectives, body(): terms = lax.all_gather(x, 'prod', axis=0, tiled=False)  30.5 us
    gather x1, local copies, waits for them, and re-layouts, request_order(): wanted = firm_map[order].reshape(holders, per_pair)  20.5 us
    psum x1, blocking collectives, body(): col_chars, col_means = lax.psum((part_chars, part_means), 'prod')  17.2 us
    all_to_all x1, blocking collectives, regroup(): lax.all_to_all(rows_out, 'prod', split_axis=0, concat_axis=0, tiled=True)  16.6 us
    dot_general x8, matrix products, consume(): jnp.dot(coef_block, scaled, precision=lax.Precision.HIGHEST)  16.6 us
  transfers between devices with their start and end apart: 4, of which 1 were waited for; matrix products, arithmetic and copies ran while one was open for 24% of the time, Pallas kernels for 0%

profile of v1, /device:TPU:0, one launch (start us, length us, event | category | flops | bytes accessed | tf_op | source)
XLA Modules:
  0.0 347.5 jit_solution(17272819656009755798)
XLA Ops:
  9.6 15.6 %while.35 = (s32[]{:T(128)}, f32[8,512]{1,0:T(8,128)S(1)}, bf16[8,512,128]{2,1,0:T(8,128)(2,1)}, bf16[2048,128]{1,0:T(8,128)(2,1)}, f32[2048]{0:T(1024)}, /*index=5*/s32[]{:T(128)}, s32[]{:T(128)}) while((s32[]{:T(128)}, f32[8,512]{1,0:T(8,128)S(1)}, bf16[8,512,128]{2,1,0:T(8,128)(2,1)}, bf16[2048,128]{1,0:T(8,128)(2,1)}, f32[2048]{0:T(1024)}, ...), condition=%wide.region_2.3_spmd, body=%wide.region_0.2_spmd.sunk | while | flops 270532608 | bytes 674385 | solution.py:78
  25.3 38.9 %pmax.7 = f32[4096]{0:T(1024)S(1)} all-reduce(f32[4096]{0:T(1024)S(1)} %bitcast.116), channel_id=1, replica_groups=mesh['cons'=4,'prod'=8] {'prod'}, use_global_device_ids=true, to_apply=%region_3.0 | all-reduce | flops 4096 | bytes 32768 | tf_op jit(solution)/shard_map/pmax | solution.py:78
  64.1 16.9 %while.36 = (s32[]{:T(128)}, f32[8,512]{1,0:T(8,128)S(1)}, bf16[8,512,128]{2,1,0:T(8,128)(2,1)}, bf16[2048,128]{1,0:T(8,128)(2,1)}, f32[2048]{0:T(1024)}, /*index=5*/f32[8,512]{1,0:T(8,128)S(1)}, s32[]{:T(128)}, s32[]{:T(128)}) while((s32[]{:T(128)}, f32[8,512]{1,0:T(8,128)S(1)}, bf16[8,512,128]{2,1,0:T(8,128)(2,1)}, ...), condition=%wide.region_6.7_spmd, body=%wide.region_4.6_spmd.sunk | while | flops 271580672 | bytes 676445 | solution.py:85
  81.1 30.5 %all-gather = f32[8,1,4096]{2,1,0:T(1,128)S(1)} all-gather(f32[1,1,4096]{2,1,0:T(1,128)S(1)} %reshape.166), channel_id=1, replica_groups=mesh['cons'=4,'prod'=8] {'prod'}, dimensions={0}, use_global_device_ids=true | all-gather | bytes 147456 | tf_op jit(solution)/shard_map/all_gather | solution.py:87
  113.5 17.2 %psum.29 = f32[256]{0:T(256)S(1)} all-reduce(f32[256]{0:T(256)S(1)} %bitcast.128), channel_id=1, replica_groups=mesh['cons'=4,'prod'=8] {'prod'}, use_global_device_ids=true, to_apply=%region_9.10 | all-reduce | flops 256 | bytes 2048 | tf_op jit(solution)/shard_map/psum | solution.py:67
  130.7 93.8 %while.37 = (s32[]{:T(128)}, f32[2048,256]{1,0:T(8,128)S(1)}, f32[2048]{0:T(1024)S(1)}, f32[2048]{0:T(1024)S(1)}, bf16[8,512,128]{2,1,0:T(8,128)(2,1)}, /*index=...) while((s32[]{:T(128)}, f32[2048,256]{1,0:T(8,128)S(1)}, ...), condition=%wide.region_12.13_spmd.clone, body=%wide.region_10.12_spmd.clone.sunk | while | flops 1027348480 | bytes 35621072 | solution.py:123
  138.4 4.0 %convolution_add_fusion.3 = f32[2048,256]{1,0:T(8,128)S(1)} fusion(bf16[512,256]{1,0:T(8,128)(2,1)S(1)} %fusion.74, f32[2048,256]{1,0:T(8,128)S(1)} %get-tuple-element.449, f32[512,2048]{1,0:T(8,128)} %copy-done.3, pred[]{:T(512)S(6)} %compare.9), kind=kOutput, calls=%fused_computation.16.clone.1 | convolution fusion | flops 538968064 | bytes 8650753 | tf_op jit(solution)/shard_map/while/body/eval_jaxpr/dot_general | solution.py:104
  150.1 4.0 %convolution_add_fusion.3 = f32[2048,256]{1,0:T(8,128)S(1)} fusion(bf16[512,256]{1,0:T(8,128)(2,1)S(1)} %fusion.74, f32[2048,256]{1,0:T(8,128)S(1)} %get-tuple-element.449, f32[512,2048]{1,0:T(8,128)} %copy-done.3, pred[]{:T(512)S(6)} %compare.9), kind=kOutput, calls=%fused_computation.16.clone.1 | convolution fusion | flops 538968064 | bytes 8650753 | tf_op jit(solution)/shard_map/while/body/eval_jaxpr/dot_general | solution.py:104
  161.9 4.0 %convolution_add_fusion.3 = f32[2048,256]{1,0:T(8,128)S(1)} fusion(bf16[512,256]{1,0:T(8,128)(2,1)S(1)} %fusion.74, f32[2048,256]{1,0:T(8,128)S(1)} %get-tuple-element.449, f32[512,2048]{1,0:T(8,128)} %copy-done.3, pred[]{:T(512)S(6)} %compare.9), kind=kOutput, calls=%fused_computation.16.clone.1 | convolution fusion | flops 538968064 | bytes 8650753 | tf_op jit(solution)/shard_map/while/body/eval_jaxpr/dot_general | solution.py:104
  173.6 4.0 %convolution_add_fusion.3 = f32[2048,256]{1,0:T(8,128)S(1)} fusion(bf16[512,256]{1,0:T(8,128)(2,1)S(1)} %fusion.74, f32[2048,256]{1,0:T(8,128)S(1)} %get-tuple-element.449, f32[512,2048]{1,0:T(8,128)} %copy-done.3, pred[]{:T(512)S(6)} %compare.9), kind=kOutput, calls=%fused_computation.16.clone.1 | convolution fusion | flops 538968064 | bytes 8650753 | tf_op jit(solution)/shard_map/while/body/eval_jaxpr/dot_general | solution.py:104
  185.3 4.0 %convolution_add_fusion.3 = f32[2048,256]{1,0:T(8,128)S(1)} fusion(bf16[512,256]{1,0:T(8,128)(2,1)S(1)} %fusion.74, f32[2048,256]{1,0:T(8,128)S(1)} %get-tuple-element.449, f32[512,2048]{1,0:T(8,128)} %copy-done.3, pred[]{:T(512)S(6)} %compare.9), kind=kOutput, calls=%fused_computation.16.clone.1 | convolution fusion | flops 538968064 | bytes 8650753 | tf_op jit(solution)/shard_map/while/body/eval_jaxpr/dot_general | solution.py:104
  197.1 4.0 %convolution_add_fusion.3 = f32[2048,256]{1,0:T(8,128)S(1)} fusion(bf16[512,256]{1,0:T(8,128)(2,1)S(1)} %fusion.74, f32[2048,256]{1,0:T(8,128)S(1)} %get-tuple-element.449, f32[512,2048]{1,0:T(8,128)} %copy-done.3, pred[]{:T(512)S(6)} %compare.9), kind=kOutput, calls=%fused_computation.16.clone.1 | convolution fusion | flops 538968064 | bytes 8650753 | tf_op jit(solution)/shard_map/while/body/eval_jaxpr/dot_general | solution.py:104
  208.8 4.0 %convolution_add_fusion.3 = f32[2048,256]{1,0:T(8,128)S(1)} fusion(bf16[512,256]{1,0:T(8,128)(2,1)S(1)} %fusion.74, f32[2048,256]{1,0:T(8,128)S(1)} %get-tuple-element.449, f32[512,2048]{1,0:T(8,128)} %copy-done.3, pred[]{:T(512)S(6)} %compare.9), kind=kOutput, calls=%fused_computation.16.clone.1 | convolution fusion | flops 538968064 | bytes 8650753 | tf_op jit(solution)/shard_map/while/body/eval_jaxpr/dot_general | solution.py:104
  220.5 4.0 %convolution_add_fusion.3 = f32[2048,256]{1,0:T(8,128)S(1)} fusion(bf16[512,256]{1,0:T(8,128)(2,1)S(1)} %fusion.74, f32[2048,256]{1,0:T(8,128)S(1)} %get-tuple-element.449, f32[512,2048]{1,0:T(8,128)} %copy-done.3, pred[]{:T(512)S(6)} %compare.9), kind=kOutput, calls=%fused_computation.16.clone.1 | convolution fusion | flops 538968064 | bytes 8650753 | tf_op jit(solution)/shard_map/while/body/eval_jaxpr/dot_general | solution.py:104
  226.4 5.0 %sort.17 = (s32[2048]{0:T(1024)}, s32[2048]{0:T(1024)S(1)}) sort(s32[2048]{0:T(1024)S(1)} %add_select_fusion, s32[2048]{0:T(1024)S(1)} %iota.12), dimensions={0}, to_apply=%region_14.15 | sort | flops 22528 | bytes 32768 | tf_op jit(solution)/shard_map/jit(argsort)/sort | solution.py:19
  231.5 20.5 %gather_fusion = s32[2048]{0:T(1024)} fusion(s32[2048]{0:T(1024)S(1)} %copy-done.1, s32[2048]{0:T(1024)S(1)} %get-tuple-element.238), kind=kCustom, calls=%fused_computation | custom fusion | bytes 24576 | tf_op jit(solution)/shard_map/gather | solution.py:20
  255.5 6.3 %all-to-all-done = s32[8,1,256]{2,1,0:T(1,128)S(1)} async-done(((s32[8,1,256]{2,1,0:T(1,128)}), s32[8,1,256]{2,1,0:T(1,128)S(1)}, u32[]{:S(2)}, u32[]{:S(2)}) %all-to-all-start) | async-done | bytes 8224 | tf_op jit(solution)/shard_map/all_to_all | solution.py:28
  261.8 10.3 %all-reduce = (f32[2048]{0:T(1024)S(1)}, f32[2048]{0:T(1024)S(1)}) all-reduce(f32[2048]{0:T(1024)S(1)} %get-tuple-element.129, f32[2048]{0:T(1024)S(1)} %get-tuple-element.132), channel_id=1, replica_groups=mesh['cons'=4,'prod'=8] {'cons'}, use_global_device_ids=true, to_apply=%region_13.14 | all-reduce | flops 4096 | bytes 32768 | tf_op jit(solution)/shard_map/psum | solution.py:127
  274.3 5.5 %gather_fusion.2 = f32[2048,64]{1,0:T(8,128)S(1)} fusion(f32[2048,64]{1,0:T(8,128)S(1)} %multiply_subtract_fusion, s32[2048]{0:T(1024)S(1)} %broadcast_clamp_fusion), kind=kCustom, calls=%fused_computation.2 | custom fusion | bytes 1056768 | tf_op jit(solution)/shard_map/jit(_take)/gather | solution.py:29
  280.1 16.6 %all_to_all.20 = f32[8,256,64]{1,2,0:T(8,128)S(1)} all-to-all(f32[8,256,64]{1,2,0:T(8,128)S(1)} %broadcast_select_fusion), channel_id=1, replica_groups=mesh['cons'=4,'prod'=8] {'prod'}, dimensions={0} | all-to-all | bytes 1048576 | tf_op jit(solution)/shard_map/all_to_all | solution.py:31
  297.1 5.8 %scatter_custom_fusion.1 = f32[2048,64]{1,0:T(8,128)S(1)} fusion(s32[2048]{0:T(1024)S(1)} %get-tuple-element.239, f32[2048,64]{1,0:T(8,128)S(1)} %bitcast.110, f32[]{:T(128)} %constant.95.clone.1), kind=kCustom, calls=%fused_computation.49 | custom fusion | bytes 524292 | tf_op jit(solution)/shard_map/scatter | solution.py:35
  305.9 11.8 %gather_fusion.1 = f32[2048]{0:T(1024)S(1)} fusion(f32[2048]{0:T(1024)S(1)} %broadcast_multiply_fusion.1, s32[2048]{0:T(1024)S(1)} %broadcast_clamp_fusion), kind=kCustom, calls=%fused_computation.1 | custom fusion | bytes 24576 | tf_op jit(solution)/shard_map/jit(_take)/gather | solution.py:30
  317.7 9.9 %all_to_all.21 = f32[8,1,256]{2,1,0:T(1,128)S(1)} all-to-all(f32[8,1,256]{2,1,0:T(1,128)S(1)} %and_select_fusion), channel_id=1, replica_groups=mesh['cons'=4,'prod'=8] {'prod'}, dimensions={0} | all-to-all | bytes 16384 | tf_op jit(solution)/shard_map/all_to_all | solution.py:32
  327.6 8.0 %scatter_custom_fusion = f32[2048]{0:T(1024)S(1)} fusion(s32[2048]{0:T(1024)S(1)} %get-tuple-element.239, f32[2048]{0:T(1024)S(1)} %bitcast.127, f32[]{:T(128)} %constant.95.clone.1), kind=kCustom, calls=%fused_computation.72 | custom fusion | bytes 8196 | tf_op jit(solution)/shard_map/scatter | solution.py:36
  (191 shorter events, 113.9 us)
Async XLA Ops:
  7.2 295.8 %copy-start = (f32[16,128,128]{2,1,0:T(8,128)S(1)}, f32[16,128,128]{2,1,0:T(8,128)}, u32[]{:S(2)}) copy-start(f32[16,128,128]{2,1,0:T(8,128)} %param.19) | copy-start | bytes 3145732
  7.2 123.5 %all-reduce.3.cloned.1.call-start = ((), (), s32[]{:S(2)}) async-start(), calls=%async_computation.4 | async-start | bytes 262144 | tf_op jit(solution)/shard_map/psum | solution.py:67
  9.5 262.6 %reduce-scatter.4.cloned.1.call-start = ((), (), s32[]{:S(2)}) async-start(), calls=%async_computation.6 | async-start | bytes 2621440
  64.1 47.6 %copy-start.4 = (f32[4096]{0:T(1024)S(1)}, f32[4096]{0:T(1024)}, u32[]{:S(2)}) copy-start(f32[4096]{0:T(1024)} %param.14) | copy-start | bytes 49156
  64.1 47.6 %copy-start.6 = (s32[256]{0:T(256)S(1)}, s32[256]{0:T(256)}, u32[]{:S(2)}) copy-start(s32[256]{0:T(256)} %param.17) | copy-start | bytes 3076
  133.0 1.9 copy-start.3
  133.0 4.0 %copy-start.5 = (f32[256,128]{1,0:T(8,128)S(1)}, f32[256,128]{1,0:T(8,128)}, u32[]{:S(2)}) copy-start(f32[256,128]{1,0:T(8,128)} %get-tuple-element.472) | copy-start | bytes 393220 | tf_op jit(solution)/shard_map/while
  144.8 1.9 copy-start.3
  144.8 4.0 %copy-start.5 = (f32[256,128]{1,0:T(8,128)S(1)}, f32[256,128]{1,0:T(8,128)}, u32[]{:S(2)}) copy-start(f32[256,128]{1,0:T(8,128)} %get-tuple-element.472) | copy-start | bytes 393220 | tf_op jit(solution)/shard_map/while
  156.5 1.9 copy-start.3
  156.5 4.0 %copy-start.5 = (f32[256,128]{1,0:T(8,128)S(1)}, f32[256,128]{1,0:T(8,128)}, u32[]{:S(2)}) copy-start(f32[256,128]{1,0:T(8,128)} %get-tuple-element.472) | copy-start | bytes 393220 | tf_op jit(solution)/shard_map/while
  168.2 1.9 copy-start.3
  168.2 4.0 %copy-start.5 = (f32[256,128]{1,0:T(8,128)S(1)}, f32[256,128]{1,0:T(8,128)}, u32[]{:S(2)}) copy-start(f32[256,128]{1,0:T(8,128)} %get-tuple-element.472) | copy-start | bytes 393220 | tf_op jit(solution)/shard_map/while
  179.9 1.9 copy-start.3
  180.0 4.0 %copy-start.5 = (f32[256,128]{1,0:T(8,128)S(1)}, f32[256,128]{1,0:T(8,128)}, u32[]{:S(2)}) copy-start(f32[256,128]{1,0:T(8,128)} %get-tuple-element.472) | copy-start | bytes 393220 | tf_op jit(solution)/shard_map/while
  191.7 1.9 copy-start.3
  191.7 4.0 %copy-start.5 = (f32[256,128]{1,0:T(8,128)S(1)}, f32[256,128]{1,0:T(8,128)}, u32[]{:S(2)}) copy-start(f32[256,128]{1,0:T(8,128)} %get-tuple-element.472) | copy-start | bytes 393220 | tf_op jit(solution)/shard_map/while
  203.4 1.9 copy-start.3
  203.4 4.0 %copy-start.5 = (f32[256,128]{1,0:T(8,128)S(1)}, f32[256,128]{1,0:T(8,128)}, u32[]{:S(2)}) copy-start(f32[256,128]{1,0:T(8,128)} %get-tuple-element.472) | copy-start | bytes 393220 | tf_op jit(solution)/shard_map/while
  215.1 1.9 copy-start.3
  215.1 4.0 %copy-start.5 = (f32[256,128]{1,0:T(8,128)S(1)}, f32[256,128]{1,0:T(8,128)}, u32[]{:S(2)}) copy-start(f32[256,128]{1,0:T(8,128)} %get-tuple-element.472) | copy-start | bytes 393220 | tf_op jit(solution)/shard_map/while
  252.0 9.8 %all-to-all-start = ((s32[8,1,256]{2,1,0:T(1,128)}), s32[8,1,256]{2,1,0:T(1,128)S(1)}, u32[]{:S(2)}, u32[]{:S(2)}) async-start(s32[8,1,256]{2,1,0:T(1,128)} %bitcast.8), calls=%async_computation | async-start | bytes 16384 | tf_op jit(solution)/shard_map/all_to_all | solution.py:28
  255.3 82.7 %all-gather.3.cloned.1.call-start = ((), (), s32[]{:S(2)}) async-start(), calls=%async_computation.5 | async-start | bytes 2621440 | tf_op jit(solution)/shard_map/all_gather | solution.py:134
  305.9 11.8 %copy-start.2 = (f32[2048]{0:T(1024)}, f32[2048]{0:T(1024)S(1)}, u32[]{:S(2)}) copy-start(f32[2048]{0:T(1024)S(1)} %broadcast_multiply_fusion.1) | copy-start | bytes 24580
  (1 other events, 1.9 us)
Sparse Core Ops, SparseCore 0:
  11.9 73.2 all-reduce.2
  226.5 29.7 reduce-scatter.3
  306.0 20.7 all-gather.2
